TPU v7x, 32 devices: a whole 2x2x4 slice. The times are simulated.
32 devices in a mesh: gx: 4 (over x, core), gy: 8 (over z, y).
Axes of the slice: x: 2, y: 2, z: 4, core: 2. Of those that a mesh axis runs over, the one named last changes fastest.
Arguments:
- sources: float32 [8, 4, 256, 1024], P('gy', 'gx'), may hold values from -6 to 6
- coeff_in: bfloat16 [8, 4, 256, 256], P('gy', 'gx'), may hold values from -0.375 to 0.375
- transfer: bfloat16 [8, 8, 4, 256, 512], P(None, 'gy', 'gx'), may hold values from -0.25 to 0.25
- coeff_out: bfloat16 [8, 4, 256, 256], P('gy', 'gx'), may hold values from -0.375 to 0.375
Outputs:
- targets: float32 [8, 4, 256, 1024], P('gy', 'gx')
All inputs are finite; a program needn't handle non-finite values.
Results may differ from a plain program's by a relative error of at most 0.015.
Values may be sent and summed in bfloat16 or wider, within the bound.
A program may use at most 64 MiB of HBM per device.

v0:
```python
import jax
import jax.numpy as jnp
from jax import lax
from jax.sharding import PartitionSpec as P

LEVELS = 8


def swapped(value, axis, bit):
    mask = 2**bit
    pairs = [(source, source ^ mask) for source in range(lax.axis_size(axis))]
    return lax.ppermute(value, axis, pairs)


def combine(own, other, weights, upper):
    rank_rows = own.shape[0]
    lower_part = jnp.where(upper, other, own)
    upper_part = jnp.where(upper, own, other)
    total = jnp.dot(weights[:, :rank_rows], lower_part, preferred_element_type=jnp.float32)
    total = total + jnp.dot(weights[:, rank_rows:], upper_part, preferred_element_type=jnp.float32)
    return total.astype(jnp.bfloat16)


def partner_half(state, level_bit, low_bits):
    if level_bit < low_bits:
        return swapped(state, "gx", level_bit)
    return swapped(state, "gy", level_bit - low_bits)


def body(sources, coeff_in, transfer, coeff_out):
    low_bits = lax.axis_size("gx").bit_length() - 1
    nbits = low_bits + lax.axis_size("gy").bit_length() - 1
    position = lax.axis_index("gy") * lax.axis_size("gx") + lax.axis_index("gx")
    source_block = sources[0, 0].astype(jnp.bfloat16)
    state = jnp.dot(coeff_in[0, 0], source_block, preferred_element_type=jnp.float32).astype(
        jnp.bfloat16
    )
    cols_count = state.shape[1]
    for level in range(LEVELS):
        level_bit = nbits - 1 - level % nbits
        upper = position >> level_bit & 1 == 1
        weights = transfer[level, 0, 0]
        middle = cols_count // 2
        first_half = state[:, :middle]
        second_half = state[:, middle:]
        other_first = partner_half(first_half, level_bit, low_bits)
        new_first = combine(first_half, other_first, weights, upper)
        other_second = partner_half(second_half, level_bit, low_bits)
        new_second = combine(second_half, other_second, weights, upper)
        state = jnp.concatenate([new_first, new_second], axis=1)
    result = jnp.dot(coeff_out[0, 0], state, preferred_element_type=jnp.float32)
    return result[None, None]


def solution(mesh):
    placed = (
        P("gy", "gx", None, None),
        P("gy", "gx", None, None),
        P(None, "gy", "gx", None, None),
        P("gy", "gx", None, None),
    )
    return jax.shard_map(
        body, mesh=mesh, in_specs=placed, out_specs=P("gy", "gx", None, None), check_vma=False
    )
```

profile of v0, /device:TPU:0, one launch (start us, length us, event | category | flops | bytes accessed | tf_op | source)
XLA Modules:
  0.0 111.1 jit_solution(3834625822285886207)
XLA Ops:
  0.0 0.9 copy-done
  0.9 1.5 %convolution_convert_fusion = bf16[256,1024]{1,0:T(8,128)(2,1)S(1)} fusion(f32[1,1,256,1024]{3,2,1,0:T(8,128)} %param.4, bf16[1,1,256,256]{3,2,1,0:T(8,128)(2,1)S(1)} %copy-done), kind=kOutput, calls=%fused_computation.1 | convolution fusion | flops 134742016 | bytes 1703936 | tf_op jit(solution)/shard_map/dot_general | solution.py:35
  2.4 0.7 fusion.156
  3.2 4.1 %collective-permute-start = (bf16[256,512]{1,0:T(8,128)(2,1)S(1)}, bf16[256,512]{1,0:T(8,128)(2,1)S(1)}, u32[]{:S(2)}, u32[]{:S(2)}) collective-permute-start(bf16[256,512]{1,0:T(8,128)(2,1)S(1)} %get-tuple-element.13), channel_id=1, source_target_pairs={{0,4},{1,5},{2,6},{3,7},{4,0},{5,1},{6,2},{7,3},{8,12},{9,13},{10,... | collective-permute-start | bytes 786440 | tf_op jit(solution)/shard_map/ppermute | solution.py:12
  7.4 23.0 %collective-permute-done.8 = bf16[256,512]{1,0:T(8,128)(2,1)S(1)} collective-permute-done((bf16[256,512]{1,0:T(8,128)(2,1)}, bf16[256,512]{1,0:T(8,128)(2,1)S(1)}, u32[]{:S(2)}, u32[]{:S(2)}) %collective-permute-start.8) | collective-permute-done | bytes 262176 | tf_op jit(solution)/shard_map/ppermute | solution.py:12
  30.7 0.3 fusion.23
  31.0 0.9 collective-permute-start.9
  31.9 0.3 fusion.82
  32.2 0.3 fusion.31
  32.5 1.3 %collective-permute-start.1 = (bf16[256,512]{0,1:T(8,128)(2,1)S(1)}, bf16[256,512]{0,1:T(8,128)(2,1)S(1)}, u32[]{:S(2)}, u32[]{:S(2)}) collective-permute-start(bf16[256,512]{0,1:T(8,128)(2,1)S(1)} %fusion.31), channel_id=1, source_target_pairs={{0,2},{1,3},{2,0},{3,1},{4,6},{5,7},{6,4},{7,5},{8,10},{9,11},{10,... | collective-permute-start | bytes 786440 | tf_op jit(solution)/shard_map/ppermute | solution.py:12
  33.7 6.5 %collective-permute-done.9 = bf16[256,512]{0,1:T(8,128)(2,1)S(1)} collective-permute-done((bf16[256,512]{0,1:T(8,128)(2,1)S(1)}, bf16[256,512]{0,1:T(8,128)(2,1)S(1)}, u32[]{:S(2)}, u32[]{:S(2)}) %collective-permute-start.9) | collective-permute-done | bytes 262176 | tf_op jit(solution)/shard_map/ppermute | solution.py:12
  40.8 1.6 %collective-permute-start.10 = (bf16[256,512]{0,1:T(8,128)(2,1)S(1)}, bf16[256,512]{0,1:T(8,128)(2,1)S(1)}, u32[]{:S(2)}, u32[]{:S(2)}) collective-permute-start(bf16[256,512]{0,1:T(8,128)(2,1)S(1)} %fusion.22), channel_id=1, source_target_pairs={{0,1},{1,0},{2,3},{3,2},{4,5},{5,4},{6,7},{7,6},{8,9},{9,8},{10,11... | collective-permute-start | bytes 786440 | tf_op jit(solution)/shard_map/ppermute | solution.py:12
  42.4 1.7 %collective-permute-done.1 = bf16[256,512]{0,1:T(8,128)(2,1)S(1)} collective-permute-done((bf16[256,512]{0,1:T(8,128)(2,1)S(1)}, bf16[256,512]{0,1:T(8,128)(2,1)S(1)}, u32[]{:S(2)}, u32[]{:S(2)}) %collective-permute-start.1) | collective-permute-done | bytes 262176 | tf_op jit(solution)/shard_map/ppermute | solution.py:12
  44.7 1.4 %collective-permute-start.2 = (bf16[256,512]{0,1:T(8,128)(2,1)S(1)}, bf16[256,512]{0,1:T(8,128)(2,1)S(1)}, u32[]{:S(2)}, u32[]{:S(2)}) collective-permute-start(bf16[256,512]{0,1:T(8,128)(2,1)S(1)} %fusion.30), channel_id=1, source_target_pairs={{0,1},{1,0},{2,3},{3,2},{4,5},{5,4},{6,7},{7,6},{8,9},{9,8},{10,11... | collective-permute-start | bytes 786440 | tf_op jit(solution)/shard_map/ppermute | solution.py:12
  46.1 2.6 %collective-permute-done.10 = bf16[256,512]{0,1:T(8,128)(2,1)S(1)} collective-permute-done((bf16[256,512]{0,1:T(8,128)(2,1)S(1)}, bf16[256,512]{0,1:T(8,128)(2,1)S(1)}, u32[]{:S(2)}, u32[]{:S(2)}) %collective-permute-start.10) | collective-permute-done | bytes 262176 | tf_op jit(solution)/shard_map/ppermute | solution.py:12
  49.2 1.8 %collective-permute-start.11 = (bf16[256,512]{0,1:T(8,128)(2,1)S(1)}, bf16[256,512]{0,1:T(8,128)(2,1)S(1)}, u32[]{:S(2)}, u32[]{:S(2)}) collective-permute-start(bf16[256,512]{0,1:T(8,128)(2,1)S(1)} %fusion.21), channel_id=1, source_target_pairs={{0,16},{8,24},{16,0},{24,8},{1,17},{9,25},{17,1},{25,9},{2,18},{10... | collective-permute-start | bytes 786440 | tf_op jit(solution)/shard_map/ppermute | solution.py:12
  51.0 1.8 %collective-permute-done.2 = bf16[256,512]{0,1:T(8,128)(2,1)S(1)} collective-permute-done((bf16[256,512]{0,1:T(8,128)(2,1)S(1)}, bf16[256,512]{0,1:T(8,128)(2,1)S(1)}, u32[]{:S(2)}, u32[]{:S(2)}) %collective-permute-start.2) | collective-permute-done | bytes 262176 | tf_op jit(solution)/shard_map/ppermute | solution.py:12
  53.4 1.6 %collective-permute-start.3 = (bf16[256,512]{0,1:T(8,128)(2,1)S(1)}, bf16[256,512]{0,1:T(8,128)(2,1)S(1)}, u32[]{:S(2)}, u32[]{:S(2)}) collective-permute-start(bf16[256,512]{0,1:T(8,128)(2,1)S(1)} %fusion.29), channel_id=1, source_target_pairs={{0,16},{8,24},{16,0},{24,8},{1,17},{9,25},{17,1},{25,9},{2,18},{10... | collective-permute-start | bytes 786440 | tf_op jit(solution)/shard_map/ppermute | solution.py:12
  55.0 1.6 %collective-permute-done.11 = bf16[256,512]{0,1:T(8,128)(2,1)S(1)} collective-permute-done((bf16[256,512]{0,1:T(8,128)(2,1)S(1)}, bf16[256,512]{0,1:T(8,128)(2,1)S(1)}, u32[]{:S(2)}, u32[]{:S(2)}) %collective-permute-start.11) | collective-permute-done | bytes 262176 | tf_op jit(solution)/shard_map/ppermute | solution.py:12
  57.2 4.0 %collective-permute-done.3 = bf16[256,512]{0,1:T(8,128)(2,1)S(1)} collective-permute-done((bf16[256,512]{0,1:T(8,128)(2,1)S(1)}, bf16[256,512]{0,1:T(8,128)(2,1)S(1)}, u32[]{:S(2)}, u32[]{:S(2)}) %collective-permute-start.3) | collective-permute-done | bytes 262176 | tf_op jit(solution)/shard_map/ppermute | solution.py:12
  62.4 1.8 %collective-permute-start.13 = (bf16[256,512]{1,0:T(8,128)(2,1)S(1)}, bf16[256,512]{1,0:T(8,128)(2,1)S(1)}, u32[]{:S(2)}, u32[]{:S(2)}) collective-permute-start(bf16[256,512]{1,0:T(8,128)(2,1)S(1)} %fusion.19), channel_id=1, source_target_pairs={{0,4},{1,5},{2,6},{3,7},{4,0},{5,1},{6,2},{7,3},{8,12},{9,13},{10,... | collective-permute-start | bytes 786440 | tf_op jit(solution)/shard_map/ppermute | solution.py:12
  64.7 1.3 %collective-permute-start.5 = (bf16[256,512]{1,0:T(8,128)(2,1)S(1)}, bf16[256,512]{1,0:T(8,128)(2,1)S(1)}, u32[]{:S(2)}, u32[]{:S(2)}) collective-permute-start(bf16[256,512]{1,0:T(8,128)(2,1)S(1)} %fusion.27), channel_id=1, source_target_pairs={{0,4},{1,5},{2,6},{3,7},{4,0},{5,1},{6,2},{7,3},{8,12},{9,13},{10,... | collective-permute-start | bytes 786440 | tf_op jit(solution)/shard_map/ppermute | solution.py:12
  66.0 17.3 %collective-permute-done.13 = bf16[256,512]{1,0:T(8,128)(2,1)S(1)} collective-permute-done((bf16[256,512]{1,0:T(8,128)(2,1)S(1)}, bf16[256,512]{1,0:T(8,128)(2,1)S(1)}, u32[]{:S(2)}, u32[]{:S(2)}) %collective-permute-start.13) | collective-permute-done | bytes 262176 | tf_op jit(solution)/shard_map/ppermute | solution.py:12
  84.0 5.0 %collective-permute-done.5 = bf16[256,512]{1,0:T(8,128)(2,1)S(1)} collective-permute-done((bf16[256,512]{1,0:T(8,128)(2,1)S(1)}, bf16[256,512]{1,0:T(8,128)(2,1)S(1)}, u32[]{:S(2)}, u32[]{:S(2)}) %collective-permute-start.5) | collective-permute-done | bytes 262176 | tf_op jit(solution)/shard_map/ppermute | solution.py:12
  89.6 5.0 %collective-permute-done.14 = bf16[256,512]{0,1:T(8,128)(2,1)S(1)} collective-permute-done((bf16[256,512]{0,1:T(8,128)(2,1)S(1)}, bf16[256,512]{0,1:T(8,128)(2,1)S(1)}, u32[]{:S(2)}, u32[]{:S(2)}) %collective-permute-start.14) | collective-permute-done | bytes 262176 | tf_op jit(solution)/shard_map/ppermute | solution.py:12
  95.1 1.2 %collective-permute-start.15 = (bf16[256,512]{0,1:T(8,128)(2,1)S(1)}, bf16[256,512]{0,1:T(8,128)(2,1)S(1)}, u32[]{:S(2)}, u32[]{:S(2)}) collective-permute-start(bf16[256,512]{0,1:T(8,128)(2,1)S(1)} %fusion.17), channel_id=1, source_target_pairs={{0,1},{1,0},{2,3},{3,2},{4,5},{5,4},{6,7},{7,6},{8,9},{9,8},{10,11... | collective-permute-start | bytes 786440 | tf_op jit(solution)/shard_map/ppermute | solution.py:12
  96.4 3.8 %collective-permute-done.6 = bf16[256,512]{0,1:T(8,128)(2,1)S(1)} collective-permute-done((bf16[256,512]{0,1:T(8,128)(2,1)S(1)}, bf16[256,512]{0,1:T(8,128)(2,1)S(1)}, u32[]{:S(2)}, u32[]{:S(2)}) %collective-permute-start.6) | collective-permute-done | bytes 262176 | tf_op jit(solution)/shard_map/ppermute | solution.py:12
  100.7 1.2 %collective-permute-start.7 = (bf16[256,512]{0,1:T(8,128)(2,1)S(1)}, bf16[256,512]{0,1:T(8,128)(2,1)S(1)}, u32[]{:S(2)}, u32[]{:S(2)}) collective-permute-start(bf16[256,512]{0,1:T(8,128)(2,1)S(1)} %fusion.25), channel_id=1, source_target_pairs={{0,1},{1,0},{2,3},{3,2},{4,5},{5,4},{6,7},{7,6},{8,9},{9,8},{10,11... | collective-permute-start | bytes 786440 | tf_op jit(solution)/shard_map/ppermute | solution.py:12
  101.9 1.5 %collective-permute-done.15 = bf16[256,512]{0,1:T(8,128)(2,1)S(1)} collective-permute-done((bf16[256,512]{0,1:T(8,128)(2,1)S(1)}, bf16[256,512]{0,1:T(8,128)(2,1)S(1)}, u32[]{:S(2)}, u32[]{:S(2)}) %collective-permute-start.15) | collective-permute-done | bytes 262176 | tf_op jit(solution)/shard_map/ppermute | solution.py:12
  103.9 5.1 %collective-permute-done.7 = bf16[256,512]{0,1:T(8,128)(2,1)S(1)} collective-permute-done((bf16[256,512]{0,1:T(8,128)(2,1)S(1)}, bf16[256,512]{0,1:T(8,128)(2,1)S(1)}, u32[]{:S(2)}, u32[]{:S(2)}) %collective-permute-start.7) | collective-permute-done | bytes 262176 | tf_op jit(solution)/shard_map/ppermute | solution.py:12
  109.5 0.3 convolution_bitcast_fusion
  109.8 1.3 %copy.9 = f32[1,1,256,1024]{3,2,1,0:T(8,128)} copy(f32[1,1,256,1024]{2,3,1,0:T(8,128)S(1)} %convolution_bitcast_fusion) | data formatting | bytes 2097152 | tf_op jit(solution)/shard_map/broadcast_in_dim | solution.py:52
  (43 shorter events, 8.1 us)
Async XLA Ops:
  0.0 0.9 copy-start
  0.0 7.3 %copy-start.1 = (bf16[8,1,1,256,512]{4,3,2,1,0:T(8,128)(2,1)S(1)}, bf16[8,1,1,256,512]{4,3,2,1,0:T(8,128)(2,1)}, u32[]{:S(2)}) copy-start(bf16[8,1,1,256,512]{4,3,2,1,0:T(8,128)(2,1)} %param.6) | copy-start | bytes 6291460
  3.2 28.7 %collective-permute-start = (bf16[256,512]{1,0:T(8,128)(2,1)S(1)}, bf16[256,512]{1,0:T(8,128)(2,1)S(1)}, u32[]{:S(2)}, u32[]{:S(2)}) collective-permute-start(bf16[256,512]{1,0:T(8,128)(2,1)S(1)} %get-tuple-element.13), channel_id=1, source_target_pairs={{0,4},{1,5},{2,6},{3,7},{4,0},{5,1},{6,2},{7,3},{8,12},{9,13},{10,... | collective-permute-start | bytes 786440 | tf_op jit(solution)/shard_map/ppermute | solution.py:12
  7.2 23.2 %collective-permute-start.8 = (bf16[256,512]{1,0:T(8,128)(2,1)}, bf16[256,512]{1,0:T(8,128)(2,1)S(1)}, u32[]{:S(2)}, u32[]{:S(2)}) collective-permute-start(bf16[256,512]{1,0:T(8,128)(2,1)} %get-tuple-element.14), channel_id=1, source_target_pairs={{0,4},{1,5},{2,6},{3,7},{4,0},{5,1},{6,2},{7,3},{8,12},{9,13},{10,... | collective-permute-start | bytes 786440 | tf_op jit(solution)/shard_map/ppermute | solution.py:12
  31.0 9.2 %collective-permute-start.9 = (bf16[256,512]{0,1:T(8,128)(2,1)S(1)}, bf16[256,512]{0,1:T(8,128)(2,1)S(1)}, u32[]{:S(2)}, u32[]{:S(2)}) collective-permute-start(bf16[256,512]{0,1:T(8,128)(2,1)S(1)} %fusion.23), channel_id=1, source_target_pairs={{0,2},{1,3},{2,0},{3,1},{4,6},{5,7},{6,4},{7,5},{8,10},{9,11},{10,... | collective-permute-start | bytes 786440 | tf_op jit(solution)/shard_map/ppermute | solution.py:12
  32.5 11.7 %collective-permute-start.1 = (bf16[256,512]{0,1:T(8,128)(2,1)S(1)}, bf16[256,512]{0,1:T(8,128)(2,1)S(1)}, u32[]{:S(2)}, u32[]{:S(2)}) collective-permute-start(bf16[256,512]{0,1:T(8,128)(2,1)S(1)} %fusion.31), channel_id=1, source_target_pairs={{0,2},{1,3},{2,0},{3,1},{4,6},{5,7},{6,4},{7,5},{8,10},{9,11},{10,... | collective-permute-start | bytes 786440 | tf_op jit(solution)/shard_map/ppermute | solution.py:12
  40.8 7.9 %collective-permute-start.10 = (bf16[256,512]{0,1:T(8,128)(2,1)S(1)}, bf16[256,512]{0,1:T(8,128)(2,1)S(1)}, u32[]{:S(2)}, u32[]{:S(2)}) collective-permute-start(bf16[256,512]{0,1:T(8,128)(2,1)S(1)} %fusion.22), channel_id=1, source_target_pairs={{0,1},{1,0},{2,3},{3,2},{4,5},{5,4},{6,7},{7,6},{8,9},{9,8},{10,11... | collective-permute-start | bytes 786440 | tf_op jit(solution)/shard_map/ppermute | solution.py:12
  44.7 8.1 %collective-permute-start.2 = (bf16[256,512]{0,1:T(8,128)(2,1)S(1)}, bf16[256,512]{0,1:T(8,128)(2,1)S(1)}, u32[]{:S(2)}, u32[]{:S(2)}) collective-permute-start(bf16[256,512]{0,1:T(8,128)(2,1)S(1)} %fusion.30), channel_id=1, source_target_pairs={{0,1},{1,0},{2,3},{3,2},{4,5},{5,4},{6,7},{7,6},{8,9},{9,8},{10,11... | collective-permute-start | bytes 786440 | tf_op jit(solution)/shard_map/ppermute | solution.py:12
  49.2 7.4 %collective-permute-start.11 = (bf16[256,512]{0,1:T(8,128)(2,1)S(1)}, bf16[256,512]{0,1:T(8,128)(2,1)S(1)}, u32[]{:S(2)}, u32[]{:S(2)}) collective-permute-start(bf16[256,512]{0,1:T(8,128)(2,1)S(1)} %fusion.21), channel_id=1, source_target_pairs={{0,16},{8,24},{16,0},{24,8},{1,17},{9,25},{17,1},{25,9},{2,18},{10... | collective-permute-start | bytes 786440 | tf_op jit(solution)/shard_map/ppermute | solution.py:12
  53.4 7.9 %collective-permute-start.3 = (bf16[256,512]{0,1:T(8,128)(2,1)S(1)}, bf16[256,512]{0,1:T(8,128)(2,1)S(1)}, u32[]{:S(2)}, u32[]{:S(2)}) collective-permute-start(bf16[256,512]{0,1:T(8,128)(2,1)S(1)} %fusion.29), channel_id=1, source_target_pairs={{0,16},{8,24},{16,0},{24,8},{1,17},{9,25},{17,1},{25,9},{2,18},{10... | collective-permute-start | bytes 786440 | tf_op jit(solution)/shard_map/ppermute | solution.py:12
  57.1 4.7 %collective-permute-start.12 = (bf16[256,512]{0,1:T(8,128)(2,1)S(1)}, bf16[256,512]{0,1:T(8,128)(2,1)S(1)}, u32[]{:S(2)}, u32[]{:S(2)}) collective-permute-start(bf16[256,512]{0,1:T(8,128)(2,1)S(1)} %fusion.20), channel_id=1, source_target_pairs={{0,8},{8,0},{16,24},{24,16},{1,9},{9,1},{17,25},{25,17},{2,10},{10... | collective-permute-start | bytes 786440 | tf_op jit(solution)/shard_map/ppermute | solution.py:12
  61.8 2.4 %collective-permute-start.4 = (bf16[256,512]{0,1:T(8,128)(2,1)S(1)}, bf16[256,512]{0,1:T(8,128)(2,1)S(1)}, u32[]{:S(2)}, u32[]{:S(2)}) collective-permute-start(bf16[256,512]{0,1:T(8,128)(2,1)S(1)} %fusion.28), channel_id=1, source_target_pairs={{0,8},{8,0},{16,24},{24,16},{1,9},{9,1},{17,25},{25,17},{2,10},{10... | collective-permute-start | bytes 786440 | tf_op jit(solution)/shard_map/ppermute | solution.py:12
  62.4 20.9 %collective-permute-start.13 = (bf16[256,512]{1,0:T(8,128)(2,1)S(1)}, bf16[256,512]{1,0:T(8,128)(2,1)S(1)}, u32[]{:S(2)}, u32[]{:S(2)}) collective-permute-start(bf16[256,512]{1,0:T(8,128)(2,1)S(1)} %fusion.19), channel_id=1, source_target_pairs={{0,4},{1,5},{2,6},{3,7},{4,0},{5,1},{6,2},{7,3},{8,12},{9,13},{10,... | collective-permute-start | bytes 786440 | tf_op jit(solution)/shard_map/ppermute | solution.py:12
  64.7 24.3 %collective-permute-start.5 = (bf16[256,512]{1,0:T(8,128)(2,1)S(1)}, bf16[256,512]{1,0:T(8,128)(2,1)S(1)}, u32[]{:S(2)}, u32[]{:S(2)}) collective-permute-start(bf16[256,512]{1,0:T(8,128)(2,1)S(1)} %fusion.27), channel_id=1, source_target_pairs={{0,4},{1,5},{2,6},{3,7},{4,0},{5,1},{6,2},{7,3},{8,12},{9,13},{10,... | collective-permute-start | bytes 786440 | tf_op jit(solution)/shard_map/ppermute | solution.py:12
  83.9 10.7 %collective-permute-start.14 = (bf16[256,512]{0,1:T(8,128)(2,1)S(1)}, bf16[256,512]{0,1:T(8,128)(2,1)S(1)}, u32[]{:S(2)}, u32[]{:S(2)}) collective-permute-start(bf16[256,512]{0,1:T(8,128)(2,1)S(1)} %fusion.18), channel_id=1, source_target_pairs={{0,2},{1,3},{2,0},{3,1},{4,6},{5,7},{6,4},{7,5},{8,10},{9,11},{10,... | collective-permute-start | bytes 786440 | tf_op jit(solution)/shard_map/ppermute | solution.py:12
  89.6 10.6 %collective-permute-start.6 = (bf16[256,512]{0,1:T(8,128)(2,1)S(1)}, bf16[256,512]{0,1:T(8,128)(2,1)S(1)}, u32[]{:S(2)}, u32[]{:S(2)}) collective-permute-start(bf16[256,512]{0,1:T(8,128)(2,1)S(1)} %fusion.26), channel_id=1, source_target_pairs={{0,2},{1,3},{2,0},{3,1},{4,6},{5,7},{6,4},{7,5},{8,10},{9,11},{10,... | collective-permute-start | bytes 786440 | tf_op jit(solution)/shard_map/ppermute | solution.py:12
  95.1 8.2 %collective-permute-start.15 = (bf16[256,512]{0,1:T(8,128)(2,1)S(1)}, bf16[256,512]{0,1:T(8,128)(2,1)S(1)}, u32[]{:S(2)}, u32[]{:S(2)}) collective-permute-start(bf16[256,512]{0,1:T(8,128)(2,1)S(1)} %fusion.17), channel_id=1, source_target_pairs={{0,1},{1,0},{2,3},{3,2},{4,5},{5,4},{6,7},{7,6},{8,9},{9,8},{10,11... | collective-permute-start | bytes 786440 | tf_op jit(solution)/shard_map/ppermute | solution.py:12
  100.7 8.3 %collective-permute-start.7 = (bf16[256,512]{0,1:T(8,128)(2,1)S(1)}, bf16[256,512]{0,1:T(8,128)(2,1)S(1)}, u32[]{:S(2)}, u32[]{:S(2)}) collective-permute-start(bf16[256,512]{0,1:T(8,128)(2,1)S(1)} %fusion.25), channel_id=1, source_target_pairs={{0,1},{1,0},{2,3},{3,2},{4,5},{5,4},{6,7},{7,6},{8,9},{9,8},{10,11... | collective-permute-start | bytes 786440 | tf_op jit(solution)/shard_map/ppermute | solution.py:12
  103.6 5.9 %copy-start.2 = (bf16[1,1,256,256]{3,2,1,0:T(8,128)(2,1)S(1)}, bf16[1,1,256,256]{3,2,1,0:T(8,128)(2,1)}, u32[]{:S(2)}) copy-start(bf16[1,1,256,256]{3,2,1,0:T(8,128)(2,1)} %param.7) | copy-start | bytes 393220
where the time goes:
time: 111 us
  waiting for transfers between devices  78.9 us (71%)
  starting transfers between devices  18.5 us (17%)
  matrix products  10.4 us (9%)
  local copies, waits for them, and re-layouts  3.1 us (3%)
    ppermute x16, waiting for transfers between devices, swapped(): return lax.ppermute(value, axis, pairs)  78.9 us
    ppermute x16, starting transfers between devices, swapped(): return lax.ppermute(value, axis, pairs)  18.5 us
    dot_general x16, matrix products, combine(): jnp.dot(weights[:, :rank_rows], lower_part, preferred_element_type=jnp.fl...  4.32 us
    dot_general x16, matrix products, combine(): jnp.dot(weights[:, rank_rows:], upper_part, preferred_element_type=jnp.fl...  4.19 us
  transfers between devices with their start and end apart: 16, of which 13 were waited for; matrix products, arithmetic and copies ran while one was open for 7% of the time, Pallas kernels for 0%

commit v1 on v0

v1 whole, which is shorter than its diff:
```python
import functools

import jax
import jax.numpy as jnp
from jax import lax
from jax.experimental import pallas as pl
from jax.experimental.pallas import tpu as pltpu
from jax.sharding import PartitionSpec as P

MESH = pl.DeviceIdType.MESH
WIDTH = 128
LAGS = (0, 1, 2, 3, 4, 5, 6, 7, 8)


def kernel(
    low_bits,
    nbits,
    sources,
    coeff_in,
    transfer,
    coeff_out,
    targets,
    src,
    inward,
    weights,
    outward,
    pairs,
    result,
    load_sem,
    src_sem,
    out_sem,
    send_sem,
    recv_sem,
):
    levels = transfer.shape[0]
    rank = coeff_in.shape[0]
    chunks = sources.shape[1] // WIDTH
    axes = {"gx": lax.axis_index("gx"), "gy": lax.axis_index("gy")}

    def place(level):
        bit = nbits - 1 - level % nbits
        axis, mask = ("gx", 2**bit) if bit < low_bits else ("gy", 2 ** (bit - low_bits))
        index = axes[axis]
        side = index // mask % 2
        return side, {axis: index + mask * (1 - 2 * side)}

    places = [place(level) for level in range(levels)]

    def load_source(k):
        cols = pl.ds(k * WIDTH, WIDTH)
        return pltpu.make_async_copy(sources.at[:, cols], src.at[k], src_sem.at[k])

    def load_weights(level):
        return pltpu.make_async_copy(transfer.at[level], weights.at[level], load_sem.at[level])

    load_inward = pltpu.make_async_copy(coeff_in, inward, load_sem.at[levels])
    load_outward = pltpu.make_async_copy(coeff_out, outward, load_sem.at[levels + 1])

    def store_result(k):
        cols = pl.ds(k * WIDTH, WIDTH)
        return pltpu.make_async_copy(result.at[k], targets.at[:, cols], out_sem.at[k])

    def exchange(level, k):
        side, partner = places[level]
        half = pairs.at[level, k, pl.ds(pl.multiple_of(side * rank, rank), rank), :]
        return pltpu.make_async_remote_copy(
            src_ref=half,
            dst_ref=half,
            send_sem=send_sem.at[level, k],
            recv_sem=recv_sem.at[level, k],
            device_id=partner,
            device_id_type=MESH,
        )

    load_inward.start()
    for k in range(chunks):
        load_source(k).start()
    for level in range(levels):
        load_weights(level).start()
    load_outward.start()

    barrier = pltpu.get_barrier_semaphore()
    distinct = range(min(levels, nbits))
    for level in distinct:
        pl.semaphore_signal(barrier, inc=1, device_id=places[level][1], device_id_type=MESH)
    pl.semaphore_wait(barrier, len(distinct))

    def emit(level, k, total):
        side = places[level][0]
        pairs[level, k, pl.ds(pl.multiple_of(side * rank, rank), rank), :] = total.astype(jnp.bfloat16)
        exchange(level, k).start()

    def stage(s, k):
        if s == 0:
            load_source(k).wait()
            total = jnp.dot(
                inward[...], src[k].astype(jnp.bfloat16), preferred_element_type=jnp.float32
            )
            emit(0, k, total)
            return
        level = s - 1
        exchange(level, k).wait_recv()
        total = jnp.dot(weights[level], pairs[level, k], preferred_element_type=jnp.float32)
        if s < levels:
            emit(s, k, total)
            return
        state = total.astype(jnp.bfloat16)
        result[k] = jnp.dot(outward[...], state, preferred_element_type=jnp.float32)
        store_result(k).start()

    lags = LAGS
    for t in range(lags[levels] + chunks):
        for s in reversed(range(levels + 1)):
            k = t - lags[s]
            if k == 0:
                if s == 0:
                    load_inward.wait()
                else:
                    load_weights(s - 1).wait()
                if s == levels:
                    load_outward.wait()
            if 0 <= k < chunks:
                stage(s, k)

    for k in range(chunks):
        for level in range(levels):
            exchange(level, k).wait_send()
        store_result(k).wait()


def body(sources, coeff_in, transfer, coeff_out):
    low_bits = lax.axis_size("gx").bit_length() - 1
    nbits = low_bits + lax.axis_size("gy").bit_length() - 1
    levels, rank = transfer.shape[0], coeff_in.shape[2]
    leaf, cols = sources.shape[2:]
    chunks = cols // WIDTH
    result = pl.pallas_call(
        functools.partial(kernel, low_bits, nbits),
        out_shape=jax.ShapeDtypeStruct((leaf, cols), jnp.float32),
        in_specs=[pl.BlockSpec(memory_space=pl.ANY)] * 4,
        out_specs=pl.BlockSpec(memory_space=pl.ANY),
        scratch_shapes=[
            pltpu.VMEM((chunks, leaf, WIDTH), jnp.float32),
            pltpu.VMEM((rank, leaf), jnp.bfloat16),
            pltpu.VMEM((levels, rank, 2 * rank), jnp.bfloat16),
            pltpu.VMEM((leaf, rank), jnp.bfloat16),
            pltpu.VMEM((levels, chunks, 2 * rank, WIDTH), jnp.bfloat16),
            pltpu.VMEM((chunks, leaf, WIDTH), jnp.float32),
            pltpu.SemaphoreType.DMA((levels + 2,)),
            pltpu.SemaphoreType.DMA((chunks,)),
            pltpu.SemaphoreType.DMA((chunks,)),
            pltpu.SemaphoreType.DMA((levels, chunks)),
            pltpu.SemaphoreType.DMA((levels, chunks)),
        ],
        compiler_params=pltpu.CompilerParams(collective_id=0, has_side_effects=True),
        name="butterfly",
    )(sources[0, 0], coeff_in[0, 0], transfer[:, 0, 0], coeff_out[0, 0])
    return result[None, None]


def solution(mesh):
    placed = (
        P("gy", "gx", None, None),
        P("gy", "gx", None, None),
        P(None, "gy", "gx", None, None),
        P("gy", "gx", None, None),
    )
    return jax.shard_map(
        body, mesh=mesh, in_specs=placed, out_specs=P("gy", "gx", None, None), check_vma=False
    )
```

time: 111 us -> 85.2 us (0.77)
  Pallas kernels: 0 us -> 82.7 us
  waiting for transfers between devices: 78.9 us -> 0 us
  starting transfers between devices: 18.5 us -> 0 us
  matrix products: 10.4 us -> 0 us
    pallas_call x0 -> x1, Pallas kernels: none -> 82.7 us  [body(): pl.pallas_call(functools.partial(kernel, low_bits, nbits), out_shape=jax....]
    ppermute x16 -> x0, waiting for transfers between devices: 78.9 us -> none  [swapped(): return lax.ppermute(value, axis, pairs)]
    ppermute x16 -> x0, starting transfers between devices: 18.5 us -> none  [swapped(): return lax.ppermute(value, axis, pairs)]
    dot_general x34 -> x0, matrix products: 10.4 us -> none  [the longest x16 4.32 us: combine(): jnp.dot(weights[:, :rank_rows], lower_part, preferred_element_type=jnp.fl...]
    unnamed x6 -> x1, local copies, waits for them, and re-layouts: 0.91 us -> 2.31 us
    broadcast_in_dim x1 -> x0, local copies, waits for them, and re-layouts: 1.31 us -> none  [body(): return result[None, None]]
  transfers between devices with their start and end apart: 16 -> 0, of which waited for: 13 -> 0; matrix products, arithmetic and copies ran while one was open for 7% -> 0% of each run, Pallas kernels for 0% -> 0%
where the time goes in v1:
time: 85.2 us; the launch traced here: 85.1 us
  Pallas kernels  82.7 us (97%)
  local copies, waits for them, and re-layouts  2.31 us (3%)
    pallas_call x1, Pallas kernels, body(): pl.pallas_call(functools.partial(kernel, low_bits, nbits), out_shape=jax....  82.7 us
    unnamed x1, local copies, waits for them, and re-layouts  2.31 us

profile of v1, /device:TPU:0, one launch (start us, length us, event | category | flops | bytes accessed | tf_op | source)
XLA Modules:
  0.0 85.1 jit_solution(3740437615132269074)
XLA Ops:
  0.0 82.7 %butterfly.1 = f32[256,1024]{1,0:T(8,128)} custom-call(f32[256,1024]{1,0:T(8,128)} %bitcast.7, bf16[256,256]{1,0:T(8,128)(2,1)} %bitcast.8, bf16[8,256,512]{2,1,0:T(8,128)(2,1)} %bitcast.6, bf16[256,256]{1,0:T(8,128)(2,1)} %bitcast.9), custom_call_target="tpu_custom_call" | custom-call | tf_op jit(solution)/shard_map/butterfly/pallas_call | solution.py:137
  82.7 2.3 %copy.6 = f32[1,1,256,1024]{3,2,1,0:T(8,128)} copy(f32[1,1,256,1024]{3,2,1,0:T(8,128)} %bitcast.5) | data formatting | bytes 2097152

commit v2 on v1

--- a/solution.py
+++ b/solution.py
@@ -9,7 +9,7 @@
 
 MESH = pl.DeviceIdType.MESH
 WIDTH = 128
-LAGS = (0, 1, 2, 3, 4, 5, 6, 7, 8)
+LAGS = (0, 2.1, 3.9, 5.3, 6.7, 7.4, 9.5, 11.3, 12.7)
 
 
 def kernel(
@@ -108,19 +108,17 @@
         result[k] = jnp.dot(outward[...], state, preferred_element_type=jnp.float32)
         store_result(k).start()
 
-    lags = LAGS
-    for t in range(lags[levels] + chunks):
-        for s in reversed(range(levels + 1)):
-            k = t - lags[s]
-            if k == 0:
-                if s == 0:
-                    load_inward.wait()
-                else:
-                    load_weights(s - 1).wait()
-                if s == levels:
-                    load_outward.wait()
-            if 0 <= k < chunks:
-                stage(s, k)
+    turns = sorted((k + LAGS[s], -s, k) for s in range(levels + 1) for k in range(chunks))
+    for _, minus, k in turns:
+        s = -minus
+        if k == 0:
+            if s == 0:
+                load_inward.wait()
+            else:
+                load_weights(s - 1).wait()
+            if s == levels:
+                load_outward.wait()
+        stage(s, k)
 
     for k in range(chunks):
         for level in range(levels):

time: 85.2 us -> 65.3 us (0.77)
  Pallas kernels: 82.7 us -> 62.8 us
    pallas_call x1, Pallas kernels: 82.7 us -> 62.8 us  [body(): pl.pallas_call(functools.partial(kernel, low_bits, nbits), out_shape=jax....]
where the time goes in v2:
time: 65.3 us; the launch traced here: 65.1 us
  Pallas kernels  62.8 us (96%)
  local copies, waits for them, and re-layouts  2.31 us (4%)
    pallas_call x1, Pallas kernels, body(): pl.pallas_call(functools.partial(kernel, low_bits, nbits), out_shape=jax....  62.8 us
    unnamed x1, local copies, waits for them, and re-layouts  2.31 us

profile of v2, /device:TPU:0, one launch (start us, length us, event | category | flops | bytes accessed | tf_op | source)
XLA Modules:
  0.0 65.1 jit_solution(8673635417876518504)
XLA Ops:
  0.0 62.8 %butterfly.1 = f32[256,1024]{1,0:T(8,128)} custom-call(f32[256,1024]{1,0:T(8,128)} %bitcast.7, bf16[256,256]{1,0:T(8,128)(2,1)} %bitcast.8, bf16[8,256,512]{2,1,0:T(8,128)(2,1)} %bitcast.6, bf16[256,256]{1,0:T(8,128)(2,1)} %bitcast.9), custom_call_target="tpu_custom_call" | custom-call | tf_op jit(solution)/shard_map/butterfly/pallas_call | solution.py:135
  62.8 2.3 %copy.6 = f32[1,1,256,1024]{3,2,1,0:T(8,128)} copy(f32[1,1,256,1024]{3,2,1,0:T(8,128)} %bitcast.5) | data formatting | bytes 2097152

commit v3 on v2

--- a/solution.py
+++ b/solution.py
@@ -9,6 +9,7 @@
 
 MESH = pl.DeviceIdType.MESH
 WIDTH = 128
+TILES = 2
 LAGS = (0, 2.1, 3.9, 5.3, 6.7, 7.4, 9.5, 11.3, 12.7)
 
 
@@ -18,12 +19,10 @@
     sources,
     coeff_in,
     transfer,
-    coeff_out,
     targets,
     src,
     inward,
     weights,
-    outward,
     pairs,
     result,
     load_sem,
@@ -54,7 +53,6 @@
         return pltpu.make_async_copy(transfer.at[level], weights.at[level], load_sem.at[level])
 
     load_inward = pltpu.make_async_copy(coeff_in, inward, load_sem.at[levels])
-    load_outward = pltpu.make_async_copy(coeff_out, outward, load_sem.at[levels + 1])
 
     def store_result(k):
         cols = pl.ds(k * WIDTH, WIDTH)
@@ -77,7 +75,6 @@
         load_source(k).start()
     for level in range(levels):
         load_weights(level).start()
-    load_outward.start()
 
     barrier = pltpu.get_barrier_semaphore()
     distinct = range(min(levels, nbits))
@@ -105,7 +102,7 @@
             emit(s, k, total)
             return
         state = total.astype(jnp.bfloat16)
-        result[k] = jnp.dot(outward[...], state, preferred_element_type=jnp.float32)
+        result[k] = state
         store_result(k).start()
 
     turns = sorted((k + LAGS[s], -s, k) for s in range(levels + 1) for k in range(chunks))
@@ -116,8 +113,6 @@
                 load_inward.wait()
             else:
                 load_weights(s - 1).wait()
-            if s == levels:
-                load_outward.wait()
         stage(s, k)
 
     for k in range(chunks):
@@ -126,25 +121,28 @@
         store_result(k).wait()
 
 
+def expand(outward, state, targets):
+    targets[...] = jnp.dot(outward[...], state[...], preferred_element_type=jnp.float32)
+
+
 def body(sources, coeff_in, transfer, coeff_out):
     low_bits = lax.axis_size("gx").bit_length() - 1
     nbits = low_bits + lax.axis_size("gy").bit_length() - 1
     levels, rank = transfer.shape[0], coeff_in.shape[2]
     leaf, cols = sources.shape[2:]
     chunks = cols // WIDTH
-    result = pl.pallas_call(
+    state = pl.pallas_call(
         functools.partial(kernel, low_bits, nbits),
-        out_shape=jax.ShapeDtypeStruct((leaf, cols), jnp.float32),
-        in_specs=[pl.BlockSpec(memory_space=pl.ANY)] * 4,
+        out_shape=jax.ShapeDtypeStruct((rank, cols), jnp.bfloat16),
+        in_specs=[pl.BlockSpec(memory_space=pl.ANY)] * 3,
         out_specs=pl.BlockSpec(memory_space=pl.ANY),
         scratch_shapes=[
             pltpu.VMEM((chunks, leaf, WIDTH), jnp.float32),
             pltpu.VMEM((rank, leaf), jnp.bfloat16),
             pltpu.VMEM((levels, rank, 2 * rank), jnp.bfloat16),
-            pltpu.VMEM((leaf, rank), jnp.bfloat16),
             pltpu.VMEM((levels, chunks, 2 * rank, WIDTH), jnp.bfloat16),
-            pltpu.VMEM((chunks, leaf, WIDTH), jnp.float32),
-            pltpu.SemaphoreType.DMA((levels + 2,)),
+            pltpu.VMEM((chunks, rank, WIDTH), jnp.bfloat16),
+            pltpu.SemaphoreType.DMA((levels + 1,)),
             pltpu.SemaphoreType.DMA((chunks,)),
             pltpu.SemaphoreType.DMA((chunks,)),
             pltpu.SemaphoreType.DMA((levels, chunks)),
@@ -152,7 +150,19 @@
         ],
         compiler_params=pltpu.CompilerParams(collective_id=0, has_side_effects=True),
         name="butterfly",
-    )(sources[0, 0], coeff_in[0, 0], transfer[:, 0, 0], coeff_out[0, 0])
+    )(sources[0, 0], coeff_in[0, 0], transfer[:, 0, 0])
+    tile = cols // TILES
+    result = pl.pallas_call(
+        expand,
+        out_shape=jax.ShapeDtypeStruct((leaf, cols), jnp.float32),
+        grid=(TILES,),
+        in_specs=[
+            pl.BlockSpec((leaf, rank), lambda i: (0, 0)),
+            pl.BlockSpec((rank, tile), lambda i: (0, i)),
+        ],
+        out_specs=pl.BlockSpec((leaf, tile), lambda i: (0, i)),
+        name="expand",
+    )(coeff_out[0, 0], state)
     return result[None, None]
 
 

time: 65.3 us -> 65.3 us (level)
  Pallas kernels: 62.8 us -> 65.2 us
  local copies, waits for them, and re-layouts: 2.31 us -> 0 us
    unnamed x1 -> x0, local copies, waits for them, and re-layouts: 2.31 us -> none
    pallas_call x0 -> x1, Pallas kernels: none -> 2.27 us  [body(): pl.pallas_call(expand, out_shape=jax.ShapeDtypeStruct((leaf, cols), jnp.f...]
where the time goes in v3:
time: 65.3 us; the launch traced here: 65.2 us
  Pallas kernels  65.2 us (100%)
    pallas_call x1, Pallas kernels, body(): pl.pallas_call(functools.partial(kernel, low_bits, nbits), out_shape=jax....  62.9 us
    pallas_call x1, Pallas kernels, body(): pl.pallas_call(expand, out_shape=jax.ShapeDtypeStruct((leaf, cols), jnp.f...  2.27 us

profile of v3, /device:TPU:0, one launch (start us, length us, event | category | flops | bytes accessed | tf_op | source)
XLA Modules:
  0.0 65.2 jit_solution(1799459307109898652)
XLA Ops:
  0.0 62.9 %butterfly.1.state = bf16[256,1024]{1,0:T(8,128)(2,1)} custom-call(f32[256,1024]{1,0:T(8,128)} %bitcast.6, bf16[256,256]{1,0:T(8,128)(2,1)} %bitcast.8, bf16[8,256,512]{2,1,0:T(8,128)(2,1)} %bitcast.5), custom_call_target="tpu_custom_call" | custom-call | tf_op jit(solution)/shard_map/butterfly/pallas_call | solution.py:134
  62.9 2.3 %expand.1 = f32[256,1024]{1,0:T(8,128)} custom-call(bf16[256,256]{1,0:T(8,128)(2,1)} %bitcast.7, bf16[256,1024]{1,0:T(8,128)(2,1)} %butterfly.1.state), custom_call_target="tpu_custom_call" | custom-call | tf_op jit(solution)/shard_map/expand/pallas_call | solution.py:155
